TPU v7x, 256 devices: a 8x8x2 block of a 8x8x16 slice. The times are simulated.
256 devices in a mesh: grp: 2 (over z), tp: 128 (over y, x, core).
Axes of the slice: x: 8, y: 8, z: 2, core: 2. Of those that a mesh axis runs over, the one named last changes fastest.
The devices are a block of a 8x8x16 slice.
Arguments:
- hidden: bfloat16 [1024, 16384], P('grp', 'tp'), parts along dimension 0, may hold values from -36 to 36
- norm_gain: float32 [16384], P('tp'), may hold values from 0.3 to 10, as said below
- prefix: int32 [2], P('grp'), parts along dimension 0, may hold values from 0 to 8192
- w_query: bfloat16 [16384, 16384], P(None, 'tp'), may hold values from -0.046875 to 0.046875
- w_kv: bfloat16 [2048, 16384], P('tp'), may hold values from -0.046875 to 0.046875
- w_scale: float32 [18432], P('tp'), may hold values from 0.25 to 4
Outputs:
- queries: bfloat16 [1024, 16384], P('grp', 'tp'), parts along dimension 0
- keys: bfloat16 [1024, 16384], P('grp', 'tp'), parts along dimension 0
- values: bfloat16 [1024, 16384], P('grp', 'tp'), parts along dimension 0
- payload: bfloat16 [1024, 16384], P('grp', 'tp'), parts along dimension 0
- row_scale: float32 [1024], P('grp'), parts along dimension 0
There are 2 independent parts, one for each index of `grp`. A program takes and returns all parts, laid end to end along the dimension named above; an argument that names none is the same for every part. Nothing has to cross between parts.
Inputs may be any that keep to these rules, and one draw needn't show every extreme that they name: `norm_gain`: positive.
All inputs are finite; a program needn't handle non-finite values. Where the computation divides by a largest or mean magnitude, that divisor is 1e-20 or more.
Results may differ from a plain program's by a relative error of at most 0.012.
Values may be sent and summed in bfloat16 or wider, within the bound.
A program may use at most 64 MiB of HBM per device.

v0:
```python
import jax
import jax.numpy as jnp
from jax import lax
from jax.sharding import PartitionSpec as P

D = 16384
HD = 128
HQ_DEV = 1
KV_COLS_DEV = 8


norm_eps = 1e-05
tiny_eps = 1e-06
rope_base = 500000.0


def turned_gather(arrays, axis, dims):
    turned = [jnp.moveaxis(a, dim, 0) for a, dim in zip(arrays, dims)]
    widths = [t[0].size for t in turned]
    both = jnp.concatenate([t.reshape(-1, w) for t, w in zip(turned, widths)], axis=1)
    whole = lax.all_gather(both, axis, axis=0, tiled=True)
    blocks = jnp.split(whole, [sum(widths[:k]) for k in range(1, len(widths))], axis=1)
    return tuple(
        (
            jnp.moveaxis(b.reshape(-1, *t.shape[1:]), 0, dim)
            for b, t, dim in zip(blocks, turned, dims)
        )
    )


def rotate(matrix, positions, offset):
    count, width = matrix.shape
    pairs = matrix.reshape(count, width // 2, 2)
    columns = offset + 2 * jnp.arange(width // 2, dtype=jnp.int32)
    pair_index = (columns % HD // 2).astype(jnp.float32)
    inverse_freq = jnp.power(jnp.float32(rope_base), -(2.0 * pair_index) / HD)
    angle = positions.astype(jnp.float32)[:, None] * inverse_freq[None, :]
    cosine = jnp.cos(angle)
    sine = jnp.sin(angle)
    first = pairs[:, :, 0]
    second = pairs[:, :, 1]
    turned = jnp.stack([first * cosine - second * sine, second * cosine + first * sine], axis=-1)
    return turned.reshape(count, width)


def kv_product(left, right_rows):
    return lax.dot_general(
        left, right_rows, (((1,), (1,)), ((), ())), preferred_element_type=jnp.float32
    )


def pick_head(gathered, head, kv_heads):
    count = gathered.shape[0]
    pieces = gathered.shape[1] // (kv_heads * KV_COLS_DEV)
    grouped = gathered.reshape(count, pieces, kv_heads, KV_COLS_DEV)
    chosen = lax.dynamic_slice_in_dim(grouped, head, 1, 2)
    return chosen.reshape(count, pieces * KV_COLS_DEV)


def local(hidden, norm_gain, prefix, w_query, w_kv, w_scale):
    count = hidden.shape[0]
    local_width = hidden.shape[1]
    whole, gains = (
        lax.all_gather(hidden, "tp", axis=1, tiled=True),
        lax.all_gather(norm_gain[None, :].astype(jnp.bfloat16), "tp", axis=1, tiled=True).astype(
            jnp.float32
        ),
    )
    widened = whole.astype(jnp.float32)
    square_sum = jnp.sum(widened * widened, axis=1)
    inverse = 1.0 / jnp.sqrt(square_sum / D + norm_eps)
    normed = widened * gains * inverse[:, None]
    row_scale = jnp.max(jnp.abs(normed), axis=1) + tiny_eps
    full_payload = (normed / row_scale[:, None]).astype(jnp.bfloat16)
    payload = lax.dynamic_slice_in_dim(
        full_payload, lax.axis_index("tp") * local_width, local_width, 1
    )
    query_raw = jnp.dot(full_payload, w_query, preferred_element_type=jnp.float32)
    kv_raw = kv_product(full_payload, w_kv)
    proj = jnp.concatenate([query_raw, kv_raw], axis=1)
    proj = proj * row_scale[:, None] * w_scale[None, :]
    qwidth = HQ_DEV * HD
    query_cols = proj[:, :qwidth]
    key_cols = proj[:, qwidth : qwidth + KV_COLS_DEV]
    value_cols = proj[:, qwidth + KV_COLS_DEV :]
    kv_heads = KV_COLS_DEV * lax.axis_size("tp") // HD
    my_index = lax.axis_index("tp")
    positions = prefix[0] + jnp.arange(count, dtype=jnp.int32)
    queries = rotate(query_cols, positions, 0).astype(jnp.bfloat16)
    rotated_keys = rotate(key_cols, positions, my_index // kv_heads * KV_COLS_DEV).astype(
        jnp.bfloat16
    )
    value_round = value_cols.astype(jnp.bfloat16)
    all_keys, all_values = turned_gather((rotated_keys, value_round), "tp", (1, 1))
    head = my_index * kv_heads // lax.axis_size("tp")
    key_head = pick_head(all_keys, head, kv_heads)
    value_head = pick_head(all_values, head, kv_heads)
    keys = jnp.tile(key_head, (1, HQ_DEV))
    values = jnp.tile(value_head, (1, HQ_DEV))
    return (queries, keys, values, payload, row_scale)


def solution(mesh):
    return jax.shard_map(
        local,
        mesh=mesh,
        in_specs=(P("grp", "tp"), P("tp"), P("grp"), P(None, "tp"), P("tp", None), P("tp")),
        out_specs=(P("grp", "tp"), P("grp", "tp"), P("grp", "tp"), P("grp", "tp"), P("grp")),
        check_vma=False,
    )
```

profile of v0, /device:TPU:513, one launch (start us, length us, event | category | flops | bytes accessed | tf_op | source)
XLA Modules:
  0.0 265.4 jit_solution(17900371330747141451)
XLA Ops:
  7.2 0.0 copy-start
  7.2 0.1 all-gather.5.cloned.1.call-start
  7.3 0.7 all-gather.5.cloned.1.call-update
  8.0 0.1 all-gather.7.cloned.1.call-start
  8.1 0.7 convert_bitcast_fusion
  8.7 58.2 %all-gather.1 = bf16[128,1,128]{2,1,0:T(2,128)(2,1)S(1)} all-gather(bf16[1,1,128]{2,1,0:T(2,128)(2,1)S(1)} %convert_bitcast_fusion), channel_id=2, replica_groups=mesh['grp'=2,'tp'=128] {'tp'}, dimensions={0}, use_global_device_ids=true | all-gather | bytes 33024 | tf_op jit(solution)/shard_map/all_gather | solution.py:65
  66.9 0.1 mul.199
  67.7 68.7 %all-gather.5.cloned.1.call-done = bf16[512,16384]{1,0:T(8,128)(2,1)} async-done(((bf16[512,128]{1,0:T(8,128)(2,1)}), bf16[512,16384]{1,0:T(8,128)(2,1)}) %all-gather.5.cloned.1.call-update) | async-done | bytes 16777232 | tf_op jit(solution)/shard_map/all_gather | solution.py:64
  136.3 0.0 copy-start.2
  136.3 7.4 %fusion.5 = f32[512]{0:T(512)S(1)} fusion(bf16[512,16384]{1,0:T(8,128)(2,1)} %all-gather.5.cloned.1.call-done), kind=kLoop, calls=%fused_computation.7 | loop fusion | flops 25165312 | bytes 16779264 | tf_op jit(solution)/shard_map/reduce_sum | solution.py:70
  143.8 3.2 %copy-done.2 = bf16[512,16384]{1,0:T(8,128)(2,1)S(1)} copy-done((bf16[512,16384]{1,0:T(8,128)(2,1)S(1)}, bf16[512,16384]{1,0:T(8,128)(2,1)}, u32[]{:S(2)}) %copy-start.2) | copy-done | bytes 16777240
  147.0 6.2 %fusion.3 = f32[512]{0:T(512)S(1)} fusion(bf16[512,16384]{1,0:T(8,128)(2,1)S(1)} %copy-done.2, f32[16384]{0:T(1024)S(1)} %bitcast.36, f32[512]{0:T(512)S(1)} %add_rsqrt_fusion), kind=kLoop, calls=%fused_computation.5 | loop fusion | flops 41942528 | bytes 16846848 | tf_op jit(solution)/shard_map/reduce_max | solution.py:73
  153.2 0.0 copy-start.4
  153.2 5.5 %fusion.4 = bf16[512,16384]{1,0:T(8,128)(2,1)S(1)} fusion(bf16[512,16384]{1,0:T(8,128)(2,1)S(1)} %copy-done.2, f32[16384]{0:T(1024)S(1)} %bitcast.37, f32[512]{0:T(512)S(1)} %broadcast_add_fusion, f32[512]{0:T(512)S(1)} %add_rsqrt_fusion), kind=kLoop, calls=%fused_computation.6 | loop fusion | flops 41943040 | bytes 33624064 | tf_op jit(solution)/shard_map/convert_element_type | solution.py:74
  158.7 0.0 copy-start.1
  158.7 5.7 %copy-done.1 = bf16[512,16384]{1,0:T(8,128)(2,1)} copy-done((bf16[512,16384]{1,0:T(8,128)(2,1)}, bf16[512,16384]{1,0:T(8,128)(2,1)S(1)}, u32[]{:S(2)}) %copy-start.1) | copy-done | bytes 16777240
  164.5 0.0 copy-done
  164.5 0.0 copy-start.3
  164.5 0.0 copy-start.5
  164.5 4.4 %fusion.30 = f32[512,16]{0,1:T(8,128)S(1)} fusion(bf16[512,16384]{1,0:T(8,128)(2,1)S(1)} %fusion.4, bf16[16,16384]{1,0:T(8,128)(2,1)S(1)} %copy-done), kind=kOutput, calls=%fused_computation.64 | convolution fusion | flops 268435456 | bytes 17334272 | tf_op jit(solution)/shard_map/dot_general | solution.py:47
  168.9 0.0 copy-done.3
  168.9 9.3 %fusion.29 = f32[512,128]{0,1:T(8,128)S(1)} fusion(bf16[512,16384]{1,0:T(8,128)(2,1)} %copy-done.1, bf16[16384,128]{1,0:T(8,128)(2,1)S(1)} %copy-done.3), kind=kOutput, calls=%fused_computation.63 | convolution fusion | flops 2147483648 | bytes 21233664 | tf_op jit(solution)/shard_map/dot_general | solution.py:78
  178.2 0.0 copy-done.4
  178.2 0.0 copy-done.5
  178.2 0.1 fusion.6
  178.3 0.1 fusion.20
  178.5 0.6 pad_maximum_fusion.1
  179.1 0.1 all-gather.7.cloned.1.call-update
  179.3 0.1 reshape.290
  179.4 0.2 fusion.27
  179.6 0.6 fusion.12
  180.2 0.1 copy.32
  180.4 0.1 convert_element_type.50
  180.4 0.8 copy.38
  181.2 1.6 constant_dynamic-slice_fusion
  182.8 72.5 %all-gather.7.cloned.1.call-done = bf16[1024,1024]{1,0:T(8,128)(2,1)} async-done(((bf16[8,1024]{1,0:T(8,128)(2,1)}), bf16[1024,1024]{1,0:T(8,128)(2,1)}) %all-gather.7.cloned.1.call-update) | async-done | bytes 2097168 | tf_op jit(solution)/shard_map/all_gather | solution.py:21
  255.3 1.7 fusion.26
  257.0 0.8 copy.39
  257.7 0.8 copy.40
  (15 shorter events, 0.2 us)
Async XLA Ops:
  7.2 157.3 %copy-start = (bf16[16,16384]{1,0:T(8,128)(2,1)S(1)}, bf16[16,16384]{1,0:T(8,128)(2,1)}, u32[]{:S(2)}) copy-start(bf16[16,16384]{1,0:T(8,128)(2,1)} %param.10) | copy-start | bytes 1572868
  7.2 129.1 %all-gather.5.cloned.1.call-start = ((), (), s32[]{:S(2)}) async-start(), calls=%async_computation | async-start | bytes 16908288 | tf_op jit(solution)/shard_map/all_gather | solution.py:64
  8.0 247.3 %all-gather.7.cloned.1.call-start = ((), (), s32[]{:S(2)}) async-start(), calls=%async_computation.1 | async-start | bytes 2113536 | tf_op jit(solution)/shard_map/all_gather | solution.py:21
  136.3 10.7 %copy-start.2 = (bf16[512,16384]{1,0:T(8,128)(2,1)S(1)}, bf16[512,16384]{1,0:T(8,128)(2,1)}, u32[]{:S(2)}) copy-start(bf16[512,16384]{1,0:T(8,128)(2,1)} %all-gather.5.cloned.1.call-done) | copy-start | bytes 50331652
  153.2 24.9 %copy-start.4 = (f32[512]{0:T(512)}, f32[512]{0:T(512)S(1)}, u32[]{:S(2)}) copy-start(f32[512]{0:T(512)S(1)} %broadcast_add_fusion) | copy-start | bytes 6148
  158.7 5.7 %copy-start.1 = (bf16[512,16384]{1,0:T(8,128)(2,1)}, bf16[512,16384]{1,0:T(8,128)(2,1)S(1)}, u32[]{:S(2)}) copy-start(bf16[512,16384]{1,0:T(8,128)(2,1)S(1)} %fusion.4) | copy-start | bytes 50331652
  164.5 4.4 %copy-start.3 = (bf16[16384,128]{1,0:T(8,128)(2,1)S(1)}, bf16[16384,128]{1,0:T(8,128)(2,1)}, u32[]{:S(2)}) copy-start(bf16[16384,128]{1,0:T(8,128)(2,1)} %param.9) | copy-start | bytes 12582916
  164.5 13.7 %copy-start.5 = (f32[144]{0:T(256)S(1)}, f32[144]{0:T(256)}, u32[]{:S(2)}) copy-start(f32[144]{0:T(256)} %param.11) | copy-start | bytes 1732
Sparse Core Ops, SparseCore 0:
  10.5 125.7 all-gather.4
  179.3 75.8 all-gather.6
where the time goes:
time: 266 us; the launch traced here: 265 us
  waiting for transfers between devices  142 us (53%)
  blocking collectives  58.2 us (22%)
  other arithmetic  21.4 us (8%)
  local copies, waits for them, and re-layouts  15.1 us (6%)
  between operations  15 us (6%)
  matrix products  13.7 us (5%)
    all_gather x1, waiting for transfers between devices, turned_gather(): whole = lax.all_gather(both, axis, axis=0, tiled=True)  72.5 us
    all_gather x1, waiting for transfers between devices, local(): lax.all_gather(hidden, 'tp', axis=1, tiled=True)  68.7 us
    all_gather x1, blocking collectives, local(): lax.all_gather(norm_gain[None, :].astype(jnp.bfloat16), 'tp', axis=1, til...  58.2 us
    unnamed x15, local copies, waits for them, and re-layouts  11.2 us
    dot_general x1, matrix products, local(): jnp.dot(full_payload, w_query, preferred_element_type=jnp.float32)  9.25 us
    reduce_sum x1, other arithmetic, local(): square_sum = jnp.sum(widened * widened, axis=1)  7.43 us
    reduce_max x1, other arithmetic, local(): row_scale = jnp.max(jnp.abs(normed), axis=1) + tiny_eps  6.23 us
    convert_element_type x1, other arithmetic, local(): full_payload = (normed / row_scale[:, None]).astype(jnp.bfloat16)  5.48 us
  transfers between devices with their start and end apart: 2, of which 2 were waited for; matrix products, arithmetic and copies ran while one was open for 2% of the time, Pallas kernels for 0%

commit v1 on v0

v1 whole, which is shorter than its diff:
```python
import functools
import heapq
import math

import jax
import jax.numpy as jnp
from jax import lax
from jax.experimental import pallas as pl
from jax.experimental.pallas import tpu as pltpu
from jax.sharding import PartitionSpec as P

HD = 128
KVC = 8
norm_eps = 1e-05
tiny_eps = 1e-06
rope_base = 500000.0

ROUNDS = 1
GROUP = 4
LEAD = 3.0
W_READY = 14.0
STEP = {"R": (0, 1), "L": (0, -1), "U": (1, 0), "D": (-1, 0)}
LINKS = "RLUD"


def plan(side, rounds, unit, lat=1.5):
    half = side // 2

    def signed(v):
        v %= side
        return v - side if v >= half else v

    def onward(kind, dy, dx, via):
        if kind in "SC":
            a, b = (dx, 0) if kind == "S" else (dy, 0)
        else:
            a, b = (dx, dy) if kind == "A" else (dy, dx)
        f1, b1, f2, b2 = ("R", "L", "U", "D") if kind in "AS" else ("U", "D", "R", "L")
        second = [f2, b2] if kind in "AB" else []
        if via is None:
            return [f1, b1] + second
        if b == 0:
            if via == f1 and a > -half:
                return [f1] + second
            if via == b1 and 0 < a < half - 1:
                return [b1] + second
            return second
        if b == -half:
            return []
        if via == f2 and (-b < half - 1 or a < 0):
            return [f2]
        if via == b2 and (b < half - 1 or (b == half - 1 and a >= 0)):
            return [b2]
        return []

    pending = {link: [] for link in LINKS}
    free = {link: 0.0 for link in LINKS}
    count = {link: 0 for link in LINKS}
    actions, heap, tick = [], [], [0]

    def push(time, what):
        tick[0] += 1
        heapq.heappush(heap, (time, tick[0], what))

    def offer(chunk, via, now):
        for link in onward(chunk[0], chunk[2], chunk[3], via):
            tick[0] += 1
            rank = -1 if chunk[0] in "SC" else chunk[1]
            heapq.heappush(pending[link], (rank, tick[0], now, chunk))
            push(now, ("link", link))

    for rnd in range(rounds):
        for kind in "AB":
            offer((kind, rnd, 0, 0), None, 0.0)
    push(0.6, ("stat", "S"))
    left = {"S": side - 1, "C": side - 1}
    arrived = {}
    seen = set()
    while heap:
        now, _, what = heapq.heappop(heap)
        if what[0] == "link":
            link = what[1]
            if not pending[link]:
                continue
            if free[link] > now + 1e-9:
                push(free[link], what)
                continue
            _, _, ready, chunk = heapq.heappop(pending[link])
            took = 0.1 if chunk[0] in "SC" else unit
            free[link] = now + took
            k = count[link]
            count[link] += 1
            actions.append((max(ready, now - LEAD), ("send", link, k, chunk)))
            oy, ox = STEP[link]
            there = (chunk[0], chunk[1], signed(chunk[2] - oy), signed(chunk[3] - ox))
            push(free[link] + lat, ("arrive", link, k, there))
            if pending[link]:
                push(free[link], what)
        elif what[0] == "arrive":
            _, link, k, chunk = what
            assert chunk not in seen
            seen.add(chunk)
            actions.append((now, what))
            offer(chunk, link, now)
            if chunk[0] in "SC":
                left[chunk[0]] -= 1
                if left[chunk[0]] == 0:
                    actions.append((now, ("total", chunk[0])))
                    if chunk[0] == "S":
                        push(now + 0.3, ("stat", "C"))
            else:
                arrived.setdefault((chunk[1], chunk[0]), []).append((now, chunk))
        elif what[0] == "stat":
            offer((what[1], 0, 0, 0), None, now)
    assert len(seen) == 2 * rounds * (side * side - 1) + 2 * (side - 1)
    tasks = []
    for (rnd, kind), got in arrived.items():
        got = [(0.0, (kind, rnd, 0, 0))] + got
        for at in range(0, len(got), GROUP):
            part = got[at : at + GROUP]
            tasks.append((part[-1][0], rnd, ("product", kind, rnd, at == 0, [c[2:] for _, c in part])))
    tasks.sort(key=lambda t: (t[0], t[1]))
    clock = W_READY
    for ready, _, task in tasks:
        clock = max(clock + 0.45, ready)
        actions.append((clock, task))
    last = {}
    for time, what in actions:
        if what[0] == "product":
            last[what[2]] = max(last.get(what[2], 0.0), time)
    end = max(t for t, _ in actions)
    for rnd, time in last.items():
        actions.append((time, ("partial", rnd)))
        actions.append((time + 1.8 if time < end - 3 else end + 1, ("share", rnd)))
    order = sorted(range(len(actions)), key=lambda i: (actions[i][0], i))
    return [actions[i][1] for i in order], count


def swap_pairs(x, axis):
    size = x.shape[axis]
    even = lax.broadcasted_iota(jnp.int32, x.shape, axis) % 2 == 0
    return jnp.where(even, pltpu.roll(x, size - 1, axis), pltpu.roll(x, 1, axis))


def frequency(columns):
    index = ((columns % HD) // 2).astype(jnp.float32)
    return jnp.exp2(index * (-2.0 * math.log2(rope_base) / HD))


def body(
    side, rounds, acts, count, width, kv_heads,
    prefix, h_ref, g_ref, ws_ref, wq_ref, wkv_ref,
    q_out, k_out, v_out, p_out, rs_out,
    xs, w_own, w_oth, kv_own, kv_oth, acc_q, acc_kv, part_q, part_kv,
    stat_row, stat_col, stat_oth, stat_t, cos_q, sin_q, share, heads,
    send_sem, recv_sem, local_sem, pair_send, pair_recv, share_send, share_recv,
):
    tokens = h_ref.shape[0]
    blocks = tokens // 128
    span = tokens // rounds
    half = span // 2
    me = lax.axis_index("tp")
    core = me % 2
    x = (me // 2) % side
    y = me // (2 * side)
    MESH = pl.DeviceIdType.MESH

    def device(yy, xx, cc):
        return {"tp": (yy * side + xx) * 2 + cc}

    partner = device(y, x, 1 - core)

    def slot_of(dy, dx):
        return ((y + dy + side) % side) * side + (x + dx + side) % side

    near = {
        link: device((y + oy + side) % side, (x + ox + side) % side, core)
        for link, (oy, ox) in STEP.items()
    }
    barrier = pltpu.get_barrier_semaphore()
    for target in list(near.values()) + [partner]:
        pl.semaphore_signal(barrier, inc=1, device_id=target, device_id_type=MESH)

    own_w = pltpu.make_async_copy(wq_ref.at[:, core], w_own, local_sem.at[0])
    own_kv = pltpu.make_async_copy(wkv_ref, kv_own, local_sem.at[1])
    own_w.start()
    own_kv.start()

    gain = g_ref[...]
    mine = slot_of(0, 0)
    for b in range(blocks):
        rows = slice(b * 128, (b + 1) * 128)
        xs[mine, rows, :] = (h_ref[rows, :].astype(jnp.float32) * gain).astype(jnp.bfloat16)

    pl.semaphore_wait(barrier, 5)

    def remote(src, dst, ssem, rsem, target):
        return pltpu.make_async_remote_copy(
            src_ref=src, dst_ref=dst, send_sem=ssem, recv_sem=rsem, device_id=target, device_id_type=MESH
        )

    give_kv = remote(wkv_ref, kv_oth, pair_send.at[0], pair_recv.at[0], partner)
    give_w = remote(wq_ref.at[:, 1 - core], w_oth, pair_send.at[1], pair_recv.at[1], partner)

    def tokens_of(kind, rnd):
        return rnd * span + (half if kind == "B" else 0)

    def place(chunk):
        kind, rnd, dy, dx = chunk
        if kind == "S":
            return stat_row.at[(x + dx + side) % side]
        if kind == "C":
            return stat_col.at[(y + dy + side) % side]
        return xs.at[slot_of(dy, dx), pl.ds(tokens_of(kind, rnd), half), :]

    def hop(link, k, chunk):
        ref = place(chunk)
        return remote(ref, ref, send_sem.at[LINKS.index(link), k], recv_sem.at[LINKS.index(link), k], near[link])

    def statistics():
        lane = lax.broadcasted_iota(jnp.int32, (128, 128), 1)
        total = jnp.zeros((128, 128), jnp.float32)
        for b in range(blocks):
            rows = slice(b * 128, (b + 1) * 128)
            wide = h_ref[rows, :].astype(jnp.float32)
            squares = jnp.sum(wide * wide, axis=1, keepdims=True)
            peak = jnp.max(jnp.abs(wide * gain), axis=1, keepdims=True)
            total = jnp.where(lane == 2 * b, squares, total)
            total = jnp.where(lane == 2 * b + 1, peak, total)
        stat_row[x] = jnp.transpose(total)[:8]

    def joined(a, b):
        even = lax.broadcasted_iota(jnp.int32, (8, 128), 0) % 2 == 0
        return jnp.where(even, a + b, jnp.maximum(a, b))

    def angles(b):
        rows = slice(b * 128, (b + 1) * 128)
        pos = prefix[0] + b * 128 + lax.broadcasted_iota(jnp.int32, (128, 128), 0)
        col = lax.broadcasted_iota(jnp.int32, (128, 128), 1)
        angle = pos.astype(jnp.float32) * frequency(col)
        sine = jnp.sin(angle)
        cos_q[rows, :] = jnp.cos(angle)
        sin_q[rows, :] = jnp.where(col % 2 == 0, -sine, sine)

    def product(kind, rnd, first, places):
        t0 = tokens_of(kind, rnd)
        slots = [slot_of(*p) for p in places]
        left = jnp.concatenate([xs[s, t0 : t0 + half, :] for s in slots], axis=1)
        right = jnp.concatenate([jnp.concatenate([w_own[s], w_oth[s]], axis=1) for s in slots], axis=0)
        out = jnp.dot(left, right, preferred_element_type=jnp.float32)
        starts = [pl.multiple_of((s * 2 + core) * width, width) for s in slots]
        rows_kv = jnp.concatenate(
            [jnp.concatenate([r[:, pl.ds(c, width)] for c in starts], axis=1) for r in (kv_own, kv_oth)], axis=0
        )
        kv = lax.dot_general(rows_kv, left, (((1,), (1,)), ((), ())), preferred_element_type=jnp.float32)
        for who in range(2):
            piece = out[:, who * HD : (who + 1) * HD]
            kvp = kv[who * 2 * KVC : (who + 1) * 2 * KVC]
            if first:
                acc_q[who, t0 : t0 + half, :] = piece
                acc_kv[who, :, t0 : t0 + half] = kvp
            else:
                acc_q[who, t0 : t0 + half, :] += piece
                acc_kv[who, :, t0 : t0 + half] += kvp

    def pair_copy(rnd, what):
        rng = pl.ds(rnd * span, span)
        if what == "kv":
            return remote(
                acc_kv.at[1, :, rng], part_kv.at[:, rng], pair_send.at[2 + rnd], pair_recv.at[2 + rnd], partner
            )
        at = 2 + rounds + rnd
        return remote(acc_q.at[1, rng, :], part_q.at[rng, :], pair_send.at[at], pair_recv.at[at], partner)

    give_stat = remote(
        stat_t, stat_oth, pair_send.at[2 + 2 * rounds], pair_recv.at[2 + 2 * rounds], partner
    )

    piece_me = me // kv_heads
    members = 2 * side * side // kv_heads
    head_to = me % kv_heads
    head_me = me // members

    def share_copy(rnd, m):
        rng = pl.ds(rnd * span, span)
        target = head_to * members + (m + me) % members
        return target, remote(
            share.at[:, rng], heads.at[piece_me, :, rng], share_send.at[rnd, m], share_recv.at[rnd, piece_me],
            {"tp": target},
        )

    ws_row = ws_ref[:, :HD]

    def share_round(rnd):
        rng = slice(rnd * span, (rnd + 1) * span)
        pair_copy(rnd, "kv").wait_recv()
        eye = lax.broadcasted_iota(jnp.int32, (2 * KVC, 2 * KVC), 0) == lax.broadcasted_iota(
            jnp.int32, (2 * KVC, 2 * KVC), 1
        )
        ws_col = jnp.sum(jnp.where(eye, ws_ref[:, HD:], 0.0), axis=1, keepdims=True)
        kv = (acc_kv[0, :, rng] + part_kv[:, rng]) * ws_col
        key, value = kv[:KVC], kv[KVC:]
        pos = prefix[0] + rnd * span + lax.broadcasted_iota(jnp.int32, (KVC, span), 1)
        row = lax.broadcasted_iota(jnp.int32, (KVC, span), 0)
        angle = pos.astype(jnp.float32) * frequency(piece_me * KVC + row)
        sine = jnp.sin(angle)
        key = key * jnp.cos(angle) + swap_pairs(key, 0) * jnp.where(row % 2 == 0, -sine, sine)
        both = jnp.concatenate([key, value], axis=0).astype(jnp.bfloat16)
        share[:, rng] = both

        @pl.when(head_to == head_me)
        def _():
            heads[piece_me, :, rng] = both

        for m in range(members):
            target, copy = share_copy(rnd, m)

            @pl.when(target != me)
            def _():
                copy.start()

    give_kv.start()
    give_w.start()
    started = weighed = False
    for act in acts:
        if act[0] == "send":
            _, link, k, chunk = act
            if chunk[0] == "S" and not started:
                started = True
                statistics()
            hop(link, k, chunk).start()
        elif act[0] == "arrive":
            _, link, k, chunk = act
            hop(link, k, chunk).wait_recv()
        elif act[0] == "total":
            if act[1] == "S":
                total = stat_row[0]
                for i in range(1, side):
                    total = joined(total, stat_row[i])
                stat_col[y] = total
                for b in range(blocks):
                    angles(b)
            else:
                total = stat_col[0]
                for i in range(1, side):
                    total = joined(total, stat_col[i])
                stat_t[...] = total
                give_stat.start()
        elif act[0] == "product":
            if not weighed:
                weighed = True
                own_w.wait()
                own_kv.wait()
                give_kv.wait_recv()
                give_w.wait_recv()
            product(*act[1:])
        elif act[0] == "partial":
            pair_copy(act[1], "kv").start()
            pair_copy(act[1], "q").start()
        elif act[0] == "share":
            share_round(act[1])

    give_stat.wait_recv()
    total = joined(stat_t[...], stat_oth[...])
    inverse = 1.0 / jnp.sqrt(total / (width * 2 * side * side) + norm_eps)
    even = lax.broadcasted_iota(jnp.int32, (8, 128), 0) % 2 == 0
    both = jnp.where(even, inverse, total * pltpu.roll(inverse, 1, 0) + tiny_eps)
    rs_out[...] = jnp.concatenate([both[2 * b + 1 : 2 * b + 2] for b in range(blocks)], axis=0)
    columns = jnp.transpose(jnp.concatenate([both, jnp.zeros((120, 128), jnp.float32)], axis=0))
    inv = [columns[:, 2 * b : 2 * b + 1] for b in range(blocks)]
    for b in range(blocks):
        rows = slice(b * 128, (b + 1) * 128)
        weighted = h_ref[rows, :].astype(jnp.float32) * gain
        p_out[rows, :] = ((weighted * inv[b]) / columns[:, 2 * b + 1 : 2 * b + 2]).astype(jnp.bfloat16)

    for rnd in range(rounds):
        pair_copy(rnd, "q").wait_recv()
    for b in range(blocks):
        rows = slice(b * 128, (b + 1) * 128)
        q = (acc_q[0, rows, :] + part_q[rows, :]) * ws_row * inv[b]
        q_out[rows, :] = (q * cos_q[rows, :] + swap_pairs(q, 1) * sin_q[rows, :]).astype(jnp.bfloat16)

    for rnd in range(rounds):
        for p in range(members):
            source = p * kv_heads + head_me
            rng = pl.ds(rnd * span, span)

            @pl.when(source != me)
            def _():
                remote(
                    heads.at[p, :, rng], heads.at[p, :, rng], share_send.at[rnd, 0], share_recv.at[rnd, p], partner
                ).wait_recv()

    for b in range(blocks):
        rows = slice(b * 128, (b + 1) * 128)
        got = [heads[p, :, rows].astype(jnp.float32) for p in range(members)]
        for out, at in ((k_out, 0), (v_out, KVC)):
            turned = jnp.transpose(jnp.concatenate([g[at : at + KVC] for g in got], axis=0))
            out[rows, :] = (turned * inv[b]).astype(jnp.bfloat16)

    for act in acts:
        if act[0] == "send":
            hop(*act[1:]).wait_send()
    give_kv.wait_send()
    give_w.wait_send()
    give_stat.wait_send()
    for rnd in range(rounds):
        pair_copy(rnd, "kv").wait_send()
        pair_copy(rnd, "q").wait_send()
        for m in range(members):
            target, copy = share_copy(rnd, m)

            @pl.when(target != me)
            def _():
                copy.wait_send()


def local(tp, hidden, norm_gain, prefix, w_query, w_kv, w_scale):
    tokens, width = hidden.shape
    side = math.isqrt(tp // 2)
    kv_heads = KVC * tp // HD
    members = tp // kv_heads
    rounds = ROUNDS
    acts, count = plan(side, rounds, 1.41 / rounds)
    most = max(count.values())
    chips = tp // 2
    bf, f32 = jnp.bfloat16, jnp.float32
    vm = pl.BlockSpec(memory_space=pltpu.VMEM)
    out = jax.ShapeDtypeStruct((tokens, HD), bf)
    DMA = pltpu.SemaphoreType.DMA
    queries, keys, values, payload, scale = pl.pallas_call(
        functools.partial(body, side, rounds, acts, count, width, kv_heads),
        out_shape=(out, out, out, jax.ShapeDtypeStruct((tokens, width), bf), jax.ShapeDtypeStruct((tokens // 128, 128), f32)),
        in_specs=[pl.BlockSpec(memory_space=pltpu.SMEM), vm, vm, vm, pl.BlockSpec(memory_space=pl.ANY), pl.BlockSpec(memory_space=pl.ANY)],
        out_specs=(vm,) * 5,
        scratch_shapes=[
            pltpu.VMEM((chips, tokens, width), bf),
            pltpu.VMEM((chips, width, HD), bf),
            pltpu.VMEM((chips, width, HD), bf),
            pltpu.VMEM(w_kv.shape, bf),
            pltpu.VMEM(w_kv.shape, bf),
            pltpu.VMEM((2, tokens, HD), f32),
            pltpu.VMEM((2, 2 * KVC, tokens), f32),
            pltpu.VMEM((tokens, HD), f32),
            pltpu.VMEM((2 * KVC, tokens), f32),
            pltpu.VMEM((side, 8, 128), f32),
            pltpu.VMEM((side, 8, 128), f32),
            pltpu.VMEM((8, 128), f32),
            pltpu.VMEM((8, 128), f32),
            pltpu.VMEM((tokens, HD), f32),
            pltpu.VMEM((tokens, HD), f32),
            pltpu.VMEM((2 * KVC, tokens), bf),
            pltpu.VMEM((members, 2 * KVC, tokens), bf),
            DMA((4, most)),
            DMA((4, most)),
            DMA((2,)),
            DMA((3 + 2 * rounds,)),
            DMA((3 + 2 * rounds,)),
            DMA((rounds, members)),
            DMA((rounds, members)),
        ],
        compiler_params=pltpu.CompilerParams(
            collective_id=0, has_side_effects=True, vmem_limit_bytes=62 * 1024 * 1024
        ),
    )(
        prefix,
        hidden,
        norm_gain.reshape(1, width),
        w_scale.reshape(1, -1),
        w_query.reshape(chips, 2, width, HD),
        w_kv,
    )
    return queries, keys, values, payload, scale.reshape(tokens)


def solution(mesh):
    return jax.shard_map(
        functools.partial(local, mesh.shape["tp"]),
        mesh=mesh,
        in_specs=(P("grp", "tp"), P("tp"), P("grp"), P(None, "tp"), P("tp", None), P("tp")),
        out_specs=(P("grp", "tp"), P("grp", "tp"), P("grp", "tp"), P("grp", "tp"), P("grp")),
        check_vma=False,
    )
```

time: 266 us -> 98.1 us (0.37)
  waiting for transfers between devices: 142 us -> 0 us
  Pallas kernels: 0 us -> 89.1 us
  blocking collectives: 58.2 us -> 0 us
  other arithmetic: 21.4 us -> 0 us
  between operations: 15 us -> 1.29 us
  matrix products: 13.7 us -> 0 us
  local copies, waits for them, and re-layouts: 15.1 us -> 7.52 us
    all_gather x2 -> x0, waiting for transfers between devices: 141 us -> none  [the longest x1 72.5 us: turned_gather(): whole = lax.all_gather(both, axis, axis=0, tiled=True)]
    pallas_call x0 -> x1, Pallas kernels: none -> 89.1 us  [local(): pl.pallas_call(functools.partial(body, side, rounds, acts, count, width,...]
    all_gather x1 -> x0, blocking collectives: 58.2 us -> none  [local(): lax.all_gather(norm_gain[None, :].astype(jnp.bfloat16), 'tp', axis=1, til...]
    dot_general x2 -> x0, matrix products: 13.7 us -> none  [the longest x1 9.25 us: local(): jnp.dot(full_payload, w_query, preferred_element_type=jnp.float32)]
    reduce_sum x1 -> x0, other arithmetic: 7.43 us -> none  [local(): square_sum = jnp.sum(widened * widened, axis=1)]
    reduce_max x1 -> x0, other arithmetic: 6.23 us -> none  [local(): row_scale = jnp.max(jnp.abs(normed), axis=1) + tiny_eps]
    convert_element_type x2 -> x0, other arithmetic: 5.48 us -> none  [the longest x1 5.48 us: local(): full_payload = (normed / row_scale[:, None]).astype(jnp.bfloat16)]
    unnamed x15 -> x5, local copies, waits for them, and re-layouts: 11.2 us -> 7.52 us
  transfers between devices with their start and end apart: 2 -> 0, of which waited for: 2 -> 0; matrix products, arithmetic and copies ran while one was open for 2% -> 0% of each run, Pallas kernels for 0% -> 0%
where the time goes in v1:
time: 98.1 us; the launch traced here: 97.9 us
  Pallas kernels  89.1 us (91%)
  local copies, waits for them, and re-layouts  7.52 us (8%)
  between operations  1.29 us (1%)
    pallas_call x1, Pallas kernels, local(): pl.pallas_call(functools.partial(body, side, rounds, acts, count, width,...  89.1 us
    unnamed x5, local copies, waits for them, and re-layouts  7.52 us

profile of v1, /device:TPU:513, one launch (start us, length us, event | category | flops | bytes accessed | tf_op | source)
XLA Modules:
  0.0 97.9 jit_solution(9629275120224019912)
XLA Ops:
  1.3 89.1 %shard_map.101 = (bf16[512,128]{1,0:T(8,128)(2,1)}, bf16[512,128]{1,0:T(8,128)(2,1)}, bf16[512,128]{1,0:T(8,128)(2,1)}, bf16[512,128]{1,0:T(8,128)(2,1)}, f32[4,128]{1,0:T(4,128)}) custom-call(s32[1]{0:T(128)S(6)} %copy.16.prefix, bf16[512,128]{1,0:T(8,128)(2,1)} %h_ref.1, f32[1,128]{1,0:T(1,128)} %bitcast.7, f32[1,144]{1,0:T(1,128)} %bitcast.6, ...), custom_call_target="tpu_custom_call" | custom-call | tf_op jit(solution)/shard_map/pallas_call | solution.py:431
  90.4 1.6 %copy.17 = bf16[512,128]{1,0:T(8,128)(2,1)} copy(bf16[512,128]{1,0:T(8,128)(2,1)} %get-tuple-element.20) | data formatting | bytes 262144
  92.0 1.6 %copy.18 = bf16[512,128]{1,0:T(8,128)(2,1)} copy(bf16[512,128]{1,0:T(8,128)(2,1)} %get-tuple-element.21) | data formatting | bytes 262144
  93.5 1.6 %copy.19 = bf16[512,128]{1,0:T(8,128)(2,1)} copy(bf16[512,128]{1,0:T(8,128)(2,1)} %get-tuple-element.22) | data formatting | bytes 262144
  95.1 1.6 %copy.20 = bf16[512,128]{1,0:T(8,128)(2,1)} copy(bf16[512,128]{1,0:T(8,128)(2,1)} %get-tuple-element.23) | data formatting | bytes 262144
  96.7 1.3 %copy.21 = f32[512]{0:T(512)} copy(f32[512]{0:T(512)} %bitcast.5) | data formatting | bytes 4096

commit v2 on v1

--- a/solution.py
+++ b/solution.py
@@ -18,7 +18,7 @@
 ROUNDS = 1
 GROUP = 4
 LEAD = 3.0
-W_READY = 14.0
+W_READY = 22.0
 STEP = {"R": (0, 1), "L": (0, -1), "U": (1, 0), "D": (-1, 0)}
 LINKS = "RLUD"
 
@@ -149,13 +149,13 @@
 
 def body(
     side, rounds, acts, count, width, kv_heads,
-    prefix, h_ref, g_ref, ws_ref, wq_ref, wkv_ref,
-    q_out, k_out, v_out, p_out, rs_out,
-    xs, w_own, w_oth, kv_own, kv_oth, acc_q, acc_kv, part_q, part_kv,
-    stat_row, stat_col, stat_oth, stat_t, cos_q, sin_q, share, heads,
+    prefix, h_in, g_in, ws_in, wq_ref, wkv_ref,
+    q_out, p_out, heads, both_out,
+    h_ref, g_ref, ws_ref, xs, w_own, w_oth, kv_own, kv_oth, acc_q, acc_kv, part_q, part_kv,
+    stat_row, stat_col, stat_oth, stat_t, cos_q, sin_q, share,
     send_sem, recv_sem, local_sem, pair_send, pair_recv, share_send, share_recv,
 ):
-    tokens = h_ref.shape[0]
+    tokens = h_in.shape[0]
     blocks = tokens // 128
     span = tokens // rounds
     half = span // 2
@@ -178,21 +178,37 @@
         for link, (oy, ox) in STEP.items()
     }
     barrier = pltpu.get_barrier_semaphore()
-    for target in list(near.values()) + [partner]:
+    for target in near.values():
         pl.semaphore_signal(barrier, inc=1, device_id=target, device_id_type=MESH)
+    ins = [
+        pltpu.make_async_copy(a, b, local_sem.at[2 + i])
+        for i, (a, b) in enumerate([(h_in, h_ref), (g_in, g_ref), (ws_in, ws_ref)])
+    ]
+    for copy in ins:
+        copy.start()
 
     own_w = pltpu.make_async_copy(wq_ref.at[:, core], w_own, local_sem.at[0])
     own_kv = pltpu.make_async_copy(wkv_ref, kv_own, local_sem.at[1])
     own_w.start()
     own_kv.start()
 
+    for copy in ins:
+        copy.wait()
     gain = g_ref[...]
     mine = slot_of(0, 0)
     for b in range(blocks):
         rows = slice(b * 128, (b + 1) * 128)
         xs[mine, rows, :] = (h_ref[rows, :].astype(jnp.float32) * gain).astype(jnp.bfloat16)
 
-    pl.semaphore_wait(barrier, 5)
+    @pl.when(core == 1)
+    def _():
+        pl.semaphore_wait(barrier, 4)
+
+    @pl.when(core == 0)
+    def _():
+        pl.semaphore_wait(barrier, 5)
+
+    pl.semaphore_signal(barrier, inc=1, device_id=partner, device_id_type=MESH)
 
     def remote(src, dst, ssem, rsem, target):
         return pltpu.make_async_remote_copy(
@@ -319,8 +335,11 @@
             def _():
                 copy.start()
 
-    give_kv.start()
-    give_w.start()
+    @pl.when(core == 0)
+    def _():
+        give_kv.start()
+        give_w.start()
+
     started = weighed = False
     for act in acts:
         if act[0] == "send":
@@ -351,6 +370,13 @@
                 weighed = True
                 own_w.wait()
                 own_kv.wait()
+
+                @pl.when(core == 1)
+                def _():
+                    pl.semaphore_wait(barrier, 1)
+                    give_kv.start()
+                    give_w.start()
+
                 give_kv.wait_recv()
                 give_w.wait_recv()
             product(*act[1:])
@@ -365,7 +391,7 @@
     inverse = 1.0 / jnp.sqrt(total / (width * 2 * side * side) + norm_eps)
     even = lax.broadcasted_iota(jnp.int32, (8, 128), 0) % 2 == 0
     both = jnp.where(even, inverse, total * pltpu.roll(inverse, 1, 0) + tiny_eps)
-    rs_out[...] = jnp.concatenate([both[2 * b + 1 : 2 * b + 2] for b in range(blocks)], axis=0)
+    both_out[...] = both
     columns = jnp.transpose(jnp.concatenate([both, jnp.zeros((120, 128), jnp.float32)], axis=0))
     inv = [columns[:, 2 * b : 2 * b + 1] for b in range(blocks)]
     for b in range(blocks):
@@ -390,13 +416,6 @@
                 remote(
                     heads.at[p, :, rng], heads.at[p, :, rng], share_send.at[rnd, 0], share_recv.at[rnd, p], partner
                 ).wait_recv()
-
-    for b in range(blocks):
-        rows = slice(b * 128, (b + 1) * 128)
-        got = [heads[p, :, rows].astype(jnp.float32) for p in range(members)]
-        for out, at in ((k_out, 0), (v_out, KVC)):
-            turned = jnp.transpose(jnp.concatenate([g[at : at + KVC] for g in got], axis=0))
-            out[rows, :] = (turned * inv[b]).astype(jnp.bfloat16)
 
     for act in acts:
         if act[0] == "send":
@@ -415,25 +434,44 @@
                 copy.wait_send()
 
 
+def finish(blocks, members, q_in, p_in, heads, both, q_out, k_out, v_out, p_out, rs_out):
+    q_out[...] = q_in[...]
+    p_out[...] = p_in[...]
+    both = both[...]
+    rs_out[...] = jnp.concatenate([both[2 * b + 1 : 2 * b + 2] for b in range(blocks)], axis=0)
+    for b in range(blocks):
+        rows = slice(b * 128, (b + 1) * 128)
+        got = [heads[p, :, rows].astype(jnp.float32) for p in range(members)]
+        inverse = both[2 * b : 2 * b + 1]
+        for out, at in ((k_out, 0), (v_out, KVC)):
+            turned = jnp.concatenate([g[at : at + KVC] for g in got], axis=0) * inverse
+            out[rows, :] = jnp.transpose(turned).astype(jnp.bfloat16)
+
+
 def local(tp, hidden, norm_gain, prefix, w_query, w_kv, w_scale):
     tokens, width = hidden.shape
     side = math.isqrt(tp // 2)
     kv_heads = KVC * tp // HD
     members = tp // kv_heads
     rounds = ROUNDS
-    acts, count = plan(side, rounds, 1.41 / rounds)
+    acts, count = plan(side, rounds, 1.41 / rounds, 2.0)
     most = max(count.values())
     chips = tp // 2
     bf, f32 = jnp.bfloat16, jnp.float32
     vm = pl.BlockSpec(memory_space=pltpu.VMEM)
     out = jax.ShapeDtypeStruct((tokens, HD), bf)
     DMA = pltpu.SemaphoreType.DMA
-    queries, keys, values, payload, scale = pl.pallas_call(
+    hbm = pl.BlockSpec(memory_space=pltpu.HBM)
+    out_p = jax.ShapeDtypeStruct((tokens, width), bf)
+    queries, payload, heads, both = pl.pallas_call(
         functools.partial(body, side, rounds, acts, count, width, kv_heads),
-        out_shape=(out, out, out, jax.ShapeDtypeStruct((tokens, width), bf), jax.ShapeDtypeStruct((tokens // 128, 128), f32)),
-        in_specs=[pl.BlockSpec(memory_space=pltpu.SMEM), vm, vm, vm, pl.BlockSpec(memory_space=pl.ANY), pl.BlockSpec(memory_space=pl.ANY)],
-        out_specs=(vm,) * 5,
+        out_shape=(out, out_p, jax.ShapeDtypeStruct((members, 2 * KVC, tokens), bf), jax.ShapeDtypeStruct((8, 128), f32)),
+        in_specs=[pl.BlockSpec(memory_space=pltpu.SMEM)] + [hbm] * 5,
+        out_specs=(vm,) * 4,
         scratch_shapes=[
+            pltpu.VMEM((tokens, width), bf),
+            pltpu.VMEM((1, width), f32),
+            pltpu.VMEM((1, w_scale.shape[0]), f32),
             pltpu.VMEM((chips, tokens, width), bf),
             pltpu.VMEM((chips, width, HD), bf),
             pltpu.VMEM((chips, width, HD), bf),
@@ -450,26 +488,37 @@
             pltpu.VMEM((tokens, HD), f32),
             pltpu.VMEM((tokens, HD), f32),
             pltpu.VMEM((2 * KVC, tokens), bf),
-            pltpu.VMEM((members, 2 * KVC, tokens), bf),
             DMA((4, most)),
             DMA((4, most)),
-            DMA((2,)),
+            DMA((6,)),
             DMA((3 + 2 * rounds,)),
             DMA((3 + 2 * rounds,)),
             DMA((rounds, members)),
             DMA((rounds, members)),
         ],
         compiler_params=pltpu.CompilerParams(
-            collective_id=0, has_side_effects=True, vmem_limit_bytes=62 * 1024 * 1024
+            collective_id=0, has_side_effects=True, vmem_limit_bytes=24 * 1024 * 1024
         ),
     )(
         prefix,
-        hidden,
-        norm_gain.reshape(1, width),
-        w_scale.reshape(1, -1),
-        w_query.reshape(chips, 2, width, HD),
-        w_kv,
+        *(
+            pltpu.with_memory_space_constraint(a, pltpu.HBM)
+            for a in (
+                hidden,
+                norm_gain.reshape(1, width),
+                w_scale.reshape(1, -1),
+                w_query.reshape(chips, 2, width, HD),
+                w_kv,
+            )
+        )
     )
+    queries, keys, values, payload, scale = pl.pallas_call(
+        functools.partial(finish, tokens // 128, members),
+        out_shape=(out, out, out, out_p, jax.ShapeDtypeStruct((tokens // 128, 128), f32)),
+        in_specs=[vm] * 4,
+        out_specs=(vm,) * 5,
+        compiler_params=pltpu.CompilerParams(vmem_limit_bytes=8 * 1024 * 1024),
+    )(queries, payload, heads, both)
     return queries, keys, values, payload, scale.reshape(tokens)
 
 

time: 98.1 us -> 88.5 us (0.902)
  local copies, waits for them, and re-layouts: 7.52 us -> 0 us
  Pallas kernels: 89.1 us -> 87 us
    unnamed x5 -> x0, local copies, waits for them, and re-layouts: 7.52 us -> none
    pallas_call x1, Pallas kernels: 89.1 us -> 86.2 us  [local(): pl.pallas_call(functools.partial(body, side, rounds, acts, count, width,...]
where the time goes in v2:
time: 88.5 us; the launch traced here: 88.3 us
  Pallas kernels  87 us (98%)
  between operations  1.29 us (1%)
    pallas_call x1, Pallas kernels, local(): pl.pallas_call(functools.partial(body, side, rounds, acts, count, width,...  86.2 us

profile of v2, /device:TPU:513, one launch (start us, length us, event | category | flops | bytes accessed | tf_op | source)
XLA Modules:
  0.0 88.3 jit_solution(3668113864974885402)
XLA Ops:
  1.3 86.2 %shard_map.101 = (bf16[512,128]{1,0:T(8,128)(2,1)S(1)}, bf16[512,128]{1,0:T(8,128)(2,1)S(1)}, bf16[16,16,512]{2,1,0:T(8,128)(2,1)S(1)}, f32[8,128]{1,0:T(8,128)S(1)}) custom-call(s32[1]{0:T(128)S(6)} %copy.11.prefix, bf16[512,128]{1,0:T(8,128)(2,1)} %h_in.1, f32[1,128]{1,0:T(1,128)} %bitcast.6, f32[1,144]{1,0:T(1,128)} %bitcast.5, ...), custom_call_target="tpu_custom_call" | custom-call | tf_op jit(solution)/shard_map/pallas_call | solution.py:466
  87.5 0.9 shard_map.102

commit v3 on v2

--- a/solution.py
+++ b/solution.py
@@ -17,13 +17,13 @@
 
 ROUNDS = 1
 GROUP = 4
-LEAD = 3.0
-W_READY = 22.0
+LEAD = 6.0
+W_READY = 28.0
 STEP = {"R": (0, 1), "L": (0, -1), "U": (1, 0), "D": (-1, 0)}
 LINKS = "RLUD"
 
 
-def plan(side, rounds, unit, lat=1.5):
+def plan(side, rounds, unit, lat=3.5):
     half = side // 2
 
     def signed(v):
@@ -65,7 +65,7 @@
     def offer(chunk, via, now):
         for link in onward(chunk[0], chunk[2], chunk[3], via):
             tick[0] += 1
-            rank = -1 if chunk[0] in "SC" else chunk[1]
+            rank = -1 if chunk[0] in "SC" else abs(chunk[2] if chunk[0] == "A" else chunk[3])
             heapq.heappush(pending[link], (rank, tick[0], now, chunk))
             push(now, ("link", link))
 
@@ -454,7 +454,7 @@
     kv_heads = KVC * tp // HD
     members = tp // kv_heads
     rounds = ROUNDS
-    acts, count = plan(side, rounds, 1.41 / rounds, 2.0)
+    acts, count = plan(side, rounds, 1.41 / rounds)
     most = max(count.values())
     chips = tp // 2
     bf, f32 = jnp.bfloat16, jnp.float32

time: 88.5 us -> 81.6 us (0.922)
  Pallas kernels: 87 us -> 80.1 us
    pallas_call x1, Pallas kernels: 86.2 us -> 79.3 us  [local(): pl.pallas_call(functools.partial(body, side, rounds, acts, count, width,...]
where the time goes in v3:
time: 81.6 us; the launch traced here: 81.4 us
  Pallas kernels  80.1 us (98%)
  between operations  1.29 us (2%)
    pallas_call x1, Pallas kernels, local(): pl.pallas_call(functools.partial(body, side, rounds, acts, count, width,...  79.3 us

profile of v3, /device:TPU:513, one launch (start us, length us, event | category | flops | bytes accessed | tf_op | source)
XLA Modules:
  0.0 81.4 jit_solution(4056721825551295217)
XLA Ops:
  1.3 79.3 %shard_map.101 = (bf16[512,128]{1,0:T(8,128)(2,1)S(1)}, bf16[512,128]{1,0:T(8,128)(2,1)S(1)}, bf16[16,16,512]{2,1,0:T(8,128)(2,1)S(1)}, f32[8,128]{1,0:T(8,128)S(1)}) custom-call(s32[1]{0:T(128)S(6)} %copy.11.prefix, bf16[512,128]{1,0:T(8,128)(2,1)} %h_in.1, f32[1,128]{1,0:T(1,128)} %bitcast.6, f32[1,144]{1,0:T(1,128)} %bitcast.5, ...), custom_call_target="tpu_custom_call" | custom-call | tf_op jit(solution)/shard_map/pallas_call | solution.py:466
  80.6 0.9 %shard_map.102 = (bf16[512,128]{1,0:T(8,128)(2,1)}, bf16[512,128]{1,0:T(8,128)(2,1)}, bf16[512,128]{1,0:T(8,128)(2,1)}, bf16[512,128]{1,0:T(8,128)(2,1)}, f32[4,128]{1,0:T(4,128)}) custom-call(bf16[512,128]{1,0:T(8,128)(2,1)S(1)} %get-tuple-element.14.q_in, bf16[512,128]{1,0:T(8,128)(2,1)S(1)} %get-tuple-element.15.p_in, ...), custom_call_target="tpu_custom_call" | custom-call | tf_op jit(solution)/shard_map/pallas_call | solution.py:515

commit v4 on v3

--- a/solution.py
+++ b/solution.py
@@ -19,11 +19,13 @@
 GROUP = 4
 LEAD = 6.0
 W_READY = 28.0
+SLAB = 64
+ANGLES_AT = 10.0
 STEP = {"R": (0, 1), "L": (0, -1), "U": (1, 0), "D": (-1, 0)}
 LINKS = "RLUD"
 
 
-def plan(side, rounds, unit, lat=3.5):
+def plan(side, rounds, unit, slabs, lat=3.5):
     half = side // 2
 
     def signed(v):
@@ -124,13 +126,17 @@
     for ready, _, task in tasks:
         clock = max(clock + 0.45, ready)
         actions.append((clock, task))
-    last = {}
-    for time, what in actions:
-        if what[0] == "product":
-            last[what[2]] = max(last.get(what[2], 0.0), time)
+    for i in range(slabs):
+        actions.append((ANGLES_AT + i * (W_READY - ANGLES_AT) / slabs, ("angles", i)))
     end = max(t for t, _ in actions)
-    for rnd, time in last.items():
-        actions.append((time, ("partial", rnd)))
+    for rnd in range(rounds):
+        ours = [a for a in actions if a[1][0] == "product" and a[1][2] == rnd]
+        final = [max((a for a in ours if a[1][1] == kind), key=lambda a: a[0]) for kind in "AB"]
+        time = max(t for t, _ in final)
+        actions = [a for a in actions if not any(a is f for f in final)]
+        for part in ("kv", "q"):
+            actions += [(time, what + (part,)) for _, what in final]
+            actions.append((time, ("partial", rnd, part)))
         actions.append((time + 1.8 if time < end - 3 else end + 1, ("share", rnd)))
     order = sorted(range(len(actions)), key=lambda i: (actions[i][0], i))
     return [actions[i][1] for i in order], count
@@ -152,7 +158,7 @@
     prefix, h_in, g_in, ws_in, wq_ref, wkv_ref,
     q_out, p_out, heads, both_out,
     h_ref, g_ref, ws_ref, xs, w_own, w_oth, kv_own, kv_oth, acc_q, acc_kv, part_q, part_kv,
-    stat_row, stat_col, stat_oth, stat_t, cos_q, sin_q, share,
+    stat_row, stat_col, stat_oth, stat_t, cos_q, sin_q, cos_k, sin_k, share,
     send_sem, recv_sem, local_sem, pair_send, pair_recv, share_send, share_recv,
 ):
     tokens = h_in.shape[0]
@@ -250,33 +256,52 @@
         return jnp.where(even, a + b, jnp.maximum(a, b))
 
     def angles(b):
-        rows = slice(b * 128, (b + 1) * 128)
-        pos = prefix[0] + b * 128 + lax.broadcasted_iota(jnp.int32, (128, 128), 0)
-        col = lax.broadcasted_iota(jnp.int32, (128, 128), 1)
+        rows = slice(b * SLAB, (b + 1) * SLAB)
+        pos = prefix[0] + b * SLAB + lax.broadcasted_iota(jnp.int32, (SLAB, HD), 0)
+        col = lax.broadcasted_iota(jnp.int32, (SLAB, HD), 1)
         angle = pos.astype(jnp.float32) * frequency(col)
         sine = jnp.sin(angle)
         cos_q[rows, :] = jnp.cos(angle)
         sin_q[rows, :] = jnp.where(col % 2 == 0, -sine, sine)
 
-    def product(kind, rnd, first, places):
+    piece_me = me // kv_heads
+    members = 2 * side * side // kv_heads
+    head_to = me % kv_heads
+    head_me = me // members
+
+    def key_angles():
+        pos = prefix[0] + lax.broadcasted_iota(jnp.int32, (KVC, tokens), 1)
+        row = lax.broadcasted_iota(jnp.int32, (KVC, tokens), 0)
+        angle = pos.astype(jnp.float32) * frequency(piece_me * KVC + row)
+        sine = jnp.sin(angle)
+        cos_k[...] = jnp.cos(angle)
+        sin_k[...] = jnp.where(row % 2 == 0, -sine, sine)
+
+    def product(kind, rnd, first, places, part="both"):
         t0 = tokens_of(kind, rnd)
         slots = [slot_of(*p) for p in places]
         left = jnp.concatenate([xs[s, t0 : t0 + half, :] for s in slots], axis=1)
-        right = jnp.concatenate([jnp.concatenate([w_own[s], w_oth[s]], axis=1) for s in slots], axis=0)
-        out = jnp.dot(left, right, preferred_element_type=jnp.float32)
+        if part != "kv":
+            right = jnp.concatenate([jnp.concatenate([w_own[s], w_oth[s]], axis=1) for s in slots], axis=0)
+            out = jnp.dot(left, right, preferred_element_type=jnp.float32)
+            for who in range(2):
+                piece = out[:, who * HD : (who + 1) * HD]
+                if first:
+                    acc_q[who, t0 : t0 + half, :] = piece
+                else:
+                    acc_q[who, t0 : t0 + half, :] += piece
+        if part == "q":
+            return
         starts = [pl.multiple_of((s * 2 + core) * width, width) for s in slots]
         rows_kv = jnp.concatenate(
             [jnp.concatenate([r[:, pl.ds(c, width)] for c in starts], axis=1) for r in (kv_own, kv_oth)], axis=0
         )
         kv = lax.dot_general(rows_kv, left, (((1,), (1,)), ((), ())), preferred_element_type=jnp.float32)
         for who in range(2):
-            piece = out[:, who * HD : (who + 1) * HD]
             kvp = kv[who * 2 * KVC : (who + 1) * 2 * KVC]
             if first:
-                acc_q[who, t0 : t0 + half, :] = piece
                 acc_kv[who, :, t0 : t0 + half] = kvp
             else:
-                acc_q[who, t0 : t0 + half, :] += piece
                 acc_kv[who, :, t0 : t0 + half] += kvp
 
     def pair_copy(rnd, what):
@@ -292,17 +317,25 @@
         stat_t, stat_oth, pair_send.at[2 + 2 * rounds], pair_recv.at[2 + 2 * rounds], partner
     )
 
-    piece_me = me // kv_heads
-    members = 2 * side * side // kv_heads
-    head_to = me % kv_heads
-    head_me = me // members
+    chips = members // 2
+    far = sorted(range(chips), key=lambda o: -min(o, chips - o))
 
     def share_copy(rnd, m):
         rng = pl.ds(rnd * span, span)
-        target = head_to * members + (m + me) % members
+        target = head_to * members + 2 * ((far[m] + me // 2) % chips) + piece_me % 2
         return target, remote(
             share.at[:, rng], heads.at[piece_me, :, rng], share_send.at[rnd, m], share_recv.at[rnd, piece_me],
             {"tp": target},
+        )
+
+    def passed_on(rnd, i):
+        rng = pl.ds(rnd * span, span)
+        p = 2 * ((far[chips - 1 - i] + y) % chips)
+        mine_p, other_p = p + core, p + 1 - core
+        return mine_p, other_p, remote(
+            heads.at[mine_p, :, rng], heads.at[mine_p, :, rng], share_send.at[rnd, chips + i], share_recv.at[rnd, mine_p], partner
+        ), remote(
+            heads.at[other_p, :, rng], heads.at[other_p, :, rng], share_send.at[rnd, chips + i], share_recv.at[rnd, other_p], partner
         )
 
     ws_row = ws_ref[:, :HD]
@@ -316,19 +349,15 @@
         ws_col = jnp.sum(jnp.where(eye, ws_ref[:, HD:], 0.0), axis=1, keepdims=True)
         kv = (acc_kv[0, :, rng] + part_kv[:, rng]) * ws_col
         key, value = kv[:KVC], kv[KVC:]
-        pos = prefix[0] + rnd * span + lax.broadcasted_iota(jnp.int32, (KVC, span), 1)
-        row = lax.broadcasted_iota(jnp.int32, (KVC, span), 0)
-        angle = pos.astype(jnp.float32) * frequency(piece_me * KVC + row)
-        sine = jnp.sin(angle)
-        key = key * jnp.cos(angle) + swap_pairs(key, 0) * jnp.where(row % 2 == 0, -sine, sine)
+        key = key * cos_k[:, rng] + swap_pairs(key, 0) * sin_k[:, rng]
         both = jnp.concatenate([key, value], axis=0).astype(jnp.bfloat16)
         share[:, rng] = both
 
-        @pl.when(head_to == head_me)
+        @pl.when((head_to == head_me) & (piece_me % 2 == core))
         def _():
             heads[piece_me, :, rng] = both
 
-        for m in range(members):
+        for m in range(chips):
             target, copy = share_copy(rnd, m)
 
             @pl.when(target != me)
@@ -347,6 +376,7 @@
             if chunk[0] == "S" and not started:
                 started = True
                 statistics()
+                key_angles()
             hop(link, k, chunk).start()
         elif act[0] == "arrive":
             _, link, k, chunk = act
@@ -357,14 +387,14 @@
                 for i in range(1, side):
                     total = joined(total, stat_row[i])
                 stat_col[y] = total
-                for b in range(blocks):
-                    angles(b)
             else:
                 total = stat_col[0]
                 for i in range(1, side):
                     total = joined(total, stat_col[i])
                 stat_t[...] = total
                 give_stat.start()
+        elif act[0] == "angles":
+            angles(act[1])
         elif act[0] == "product":
             if not weighed:
                 weighed = True
@@ -381,8 +411,7 @@
                 give_w.wait_recv()
             product(*act[1:])
         elif act[0] == "partial":
-            pair_copy(act[1], "kv").start()
-            pair_copy(act[1], "q").start()
+            pair_copy(act[1], act[2]).start()
         elif act[0] == "share":
             share_round(act[1])
 
@@ -406,17 +435,6 @@
         q = (acc_q[0, rows, :] + part_q[rows, :]) * ws_row * inv[b]
         q_out[rows, :] = (q * cos_q[rows, :] + swap_pairs(q, 1) * sin_q[rows, :]).astype(jnp.bfloat16)
 
-    for rnd in range(rounds):
-        for p in range(members):
-            source = p * kv_heads + head_me
-            rng = pl.ds(rnd * span, span)
-
-            @pl.when(source != me)
-            def _():
-                remote(
-                    heads.at[p, :, rng], heads.at[p, :, rng], share_send.at[rnd, 0], share_recv.at[rnd, p], partner
-                ).wait_recv()
-
     for act in acts:
         if act[0] == "send":
             hop(*act[1:]).wait_send()
@@ -426,7 +444,22 @@
     for rnd in range(rounds):
         pair_copy(rnd, "kv").wait_send()
         pair_copy(rnd, "q").wait_send()
-        for m in range(members):
+
+    for rnd in range(rounds):
+        for i in range(chips):
+            p, _, copy, _ = passed_on(rnd, i)
+
+            @pl.when(p * kv_heads + head_me != me)
+            def _():
+                copy.wait_recv()
+
+            copy.start()
+        for i in range(chips):
+            passed_on(rnd, i)[3].wait_recv()
+        for i in range(chips):
+            passed_on(rnd, i)[2].wait_send()
+    for rnd in range(rounds):
+        for m in range(chips):
             target, copy = share_copy(rnd, m)
 
             @pl.when(target != me)
@@ -454,7 +487,7 @@
     kv_heads = KVC * tp // HD
     members = tp // kv_heads
     rounds = ROUNDS
-    acts, count = plan(side, rounds, 1.41 / rounds)
+    acts, count = plan(side, rounds, 1.41 / rounds, tokens // SLAB)
     most = max(count.values())
     chips = tp // 2
     bf, f32 = jnp.bfloat16, jnp.float32
@@ -487,6 +520,8 @@
             pltpu.VMEM((8, 128), f32),
             pltpu.VMEM((tokens, HD), f32),
             pltpu.VMEM((tokens, HD), f32),
+            pltpu.VMEM((KVC, tokens), f32),
+            pltpu.VMEM((KVC, tokens), f32),
             pltpu.VMEM((2 * KVC, tokens), bf),
             DMA((4, most)),
             DMA((4, most)),

time: 81.6 us -> 79.8 us (0.978)
  Pallas kernels: 80.1 us -> 78.4 us
    pallas_call x1, Pallas kernels: 79.3 us -> 77.5 us  [local(): pl.pallas_call(functools.partial(body, side, rounds, acts, count, width,...]
where the time goes in v4:
time: 79.8 us; the launch traced here: 79.7 us
  Pallas kernels  78.4 us (98%)
  between operations  1.29 us (2%)
    pallas_call x1, Pallas kernels, local(): pl.pallas_call(functools.partial(body, side, rounds, acts, count, width,...  77.5 us

profile of v4, /device:TPU:513, one launch (start us, length us, event | category | flops | bytes accessed | tf_op | source)
XLA Modules:
  0.0 79.7 jit_solution(2112469795590342997)
XLA Ops:
  1.3 77.5 %shard_map.101 = (bf16[512,128]{1,0:T(8,128)(2,1)S(1)}, bf16[512,128]{1,0:T(8,128)(2,1)S(1)}, bf16[16,16,512]{2,1,0:T(8,128)(2,1)S(1)}, f32[8,128]{1,0:T(8,128)S(1)}) custom-call(s32[1]{0:T(128)S(6)} %copy.11.prefix, bf16[512,128]{1,0:T(8,128)(2,1)} %h_in.1, f32[1,128]{1,0:T(1,128)} %bitcast.6, f32[1,144]{1,0:T(1,128)} %bitcast.5, ...), custom_call_target="tpu_custom_call" | custom-call | tf_op jit(solution)/shard_map/pallas_call | solution.py:499
  78.8 0.9 %shard_map.102 = (bf16[512,128]{1,0:T(8,128)(2,1)}, bf16[512,128]{1,0:T(8,128)(2,1)}, bf16[512,128]{1,0:T(8,128)(2,1)}, bf16[512,128]{1,0:T(8,128)(2,1)}, f32[4,128]{1,0:T(4,128)}) custom-call(bf16[512,128]{1,0:T(8,128)(2,1)S(1)} %get-tuple-element.14.q_in, bf16[512,128]{1,0:T(8,128)(2,1)S(1)} %get-tuple-element.15.p_in, ...), custom_call_target="tpu_custom_call" | custom-call | tf_op jit(solution)/shard_map/pallas_call | solution.py:550

commit v5 on v4

--- a/solution.py
+++ b/solution.py
@@ -364,6 +364,21 @@
             def _():
                 copy.start()
 
+    def scales():
+        give_stat.wait_recv()
+        total = joined(stat_t[...], stat_oth[...])
+        inverse = 1.0 / jnp.sqrt(total / (width * 2 * side * side) + norm_eps)
+        even = lax.broadcasted_iota(jnp.int32, (8, 128), 0) % 2 == 0
+        both = jnp.where(even, inverse, total * pltpu.roll(inverse, 1, 0) + tiny_eps)
+        both_out[...] = both
+        columns = jnp.transpose(jnp.concatenate([both, jnp.zeros((120, 128), jnp.float32)], axis=0))
+        inv = [columns[:, 2 * b : 2 * b + 1] for b in range(blocks)]
+        for b in range(blocks):
+            rows = slice(b * 128, (b + 1) * 128)
+            weighted = h_ref[rows, :].astype(jnp.float32) * gain
+            p_out[rows, :] = ((weighted * inv[b]) / columns[:, 2 * b + 1 : 2 * b + 2]).astype(jnp.bfloat16)
+        return inv
+
     @pl.when(core == 0)
     def _():
         give_kv.start()
@@ -413,20 +428,9 @@
         elif act[0] == "partial":
             pair_copy(act[1], act[2]).start()
         elif act[0] == "share":
+            if act[1] == rounds - 1:
+                inv = scales()
             share_round(act[1])
-
-    give_stat.wait_recv()
-    total = joined(stat_t[...], stat_oth[...])
-    inverse = 1.0 / jnp.sqrt(total / (width * 2 * side * side) + norm_eps)
-    even = lax.broadcasted_iota(jnp.int32, (8, 128), 0) % 2 == 0
-    both = jnp.where(even, inverse, total * pltpu.roll(inverse, 1, 0) + tiny_eps)
-    both_out[...] = both
-    columns = jnp.transpose(jnp.concatenate([both, jnp.zeros((120, 128), jnp.float32)], axis=0))
-    inv = [columns[:, 2 * b : 2 * b + 1] for b in range(blocks)]
-    for b in range(blocks):
-        rows = slice(b * 128, (b + 1) * 128)
-        weighted = h_ref[rows, :].astype(jnp.float32) * gain
-        p_out[rows, :] = ((weighted * inv[b]) / columns[:, 2 * b + 1 : 2 * b + 2]).astype(jnp.bfloat16)
 
     for rnd in range(rounds):
         pair_copy(rnd, "q").wait_recv()

time: 79.8 us -> 79.5 us (level)
  no operation moved by 1% of the time
where the time goes in v5:
time: 79.5 us; the launch traced here: 79.3 us
  Pallas kernels  78.1 us (98%)
  between operations  1.29 us (2%)
    pallas_call x1, Pallas kernels, local(): pl.pallas_call(functools.partial(body, side, rounds, acts, count, width,...  77.2 us

profile of v5, /device:TPU:513, one launch (start us, length us, event | category | flops | bytes accessed | tf_op | source)
XLA Modules:
  0.0 79.3 jit_solution(3816479071942890414)
XLA Ops:
  1.3 77.2 %shard_map.101 = (bf16[512,128]{1,0:T(8,128)(2,1)S(1)}, bf16[512,128]{1,0:T(8,128)(2,1)S(1)}, bf16[16,16,512]{2,1,0:T(8,128)(2,1)S(1)}, f32[8,128]{1,0:T(8,128)S(1)}) custom-call(s32[1]{0:T(128)S(6)} %copy.11.prefix, bf16[512,128]{1,0:T(8,128)(2,1)} %h_in.1, f32[1,128]{1,0:T(1,128)} %bitcast.6, f32[1,144]{1,0:T(1,128)} %bitcast.5, ...), custom_call_target="tpu_custom_call" | custom-call | tf_op jit(solution)/shard_map/pallas_call | solution.py:503
  78.5 0.9 %shard_map.102 = (bf16[512,128]{1,0:T(8,128)(2,1)}, bf16[512,128]{1,0:T(8,128)(2,1)}, bf16[512,128]{1,0:T(8,128)(2,1)}, bf16[512,128]{1,0:T(8,128)(2,1)}, f32[4,128]{1,0:T(4,128)}) custom-call(bf16[512,128]{1,0:T(8,128)(2,1)S(1)} %get-tuple-element.14.q_in, bf16[512,128]{1,0:T(8,128)(2,1)S(1)} %get-tuple-element.15.p_in, ...), custom_call_target="tpu_custom_call" | custom-call | tf_op jit(solution)/shard_map/pallas_call | solution.py:554
